TPU v7x, 32 devices: a whole 2x2x4 slice. The times are simulated.
32 devices in a mesh: wl: 4 (over x, core), row: 4 (over z), col: 2 (over y).
Axes of the slice: x: 2, y: 2, z: 4, core: 2. Of those that a mesh axis runs over, the one named last changes fastest.
Arguments:
- cotangent: bfloat16 [4, 2, 4096, 4096], P('wl', None, 'row', 'col'), may hold values from -6 to 6
- incident: bfloat16 [4, 4096, 4096], P('wl', 'row', 'col'), may hold values from 0.5 to 1.5
- aperture_tiles: int32 [32, 32], P('row', 'col'), may hold values 0 or 1
- charge: int32 [4], P('wl'), may hold values from 2 to 8
- wl_index: int32 [4], P('wl'), may hold values from 0 to 16
Outputs:
- gradient: bfloat16 [4096, 4096], P('row', 'col')
All inputs are finite; a program needn't handle non-finite values. No bound on the sum of `aperture_tiles` on one device may be relied on, other than what follows from the above.
Results may differ from a plain program's by a relative error of at most 0.013.
Values may be sent and summed in bfloat16 or wider, within the bound.
No kernel may reach another device: no remote copies, remote signals or barrier semaphores. Data moves between devices by JAX's collectives and lax.ppermute only.
A program may use at most 128 MiB of HBM per device.

v0:
```python
import math
import jax
import jax.numpy as jnp
from jax import lax
from jax.sharding import PartitionSpec as P

M = 512


def phase_grid(offset, amount, extent, size_m, index_value, transpose):
    pupil_pos = 2 * (offset + jnp.arange(amount, dtype=jnp.int32)) - extent + 1
    focal_pos = 2 * jnp.arange(size_m, dtype=jnp.int32) - size_m + 1
    if transpose:
        product = focal_pos[:, None] * pupil_pos[None, :]
    else:
        product = pupil_pos[:, None] * focal_pos[None, :]
    period = size_m * (32 + index_value)
    remainder = jnp.remainder(4 * product, period)
    return remainder.astype(jnp.float32) * (jnp.float32(2.0 * math.pi) / period.astype(jnp.float32))


def vortex(focal_re, focal_im, charge_value):
    size_m = focal_re.shape[1]
    row_count = focal_re.shape[0]
    row_pos = (2 * jnp.arange(row_count, dtype=jnp.int32) - size_m + 1).astype(jnp.float32)
    col_pos = (2 * jnp.arange(size_m, dtype=jnp.int32) - size_m + 1).astype(jnp.float32)
    angles = jnp.arctan2(col_pos[None, :], row_pos[:, None]) * charge_value.astype(jnp.float32)
    cosine = jnp.cos(angles)
    sine_value = jnp.sin(angles)
    turned_re = focal_re * cosine + focal_im * sine_value
    turned_im = focal_im * cosine - focal_re * sine_value
    return jnp.concatenate([turned_re, turned_im], axis=1).astype(jnp.bfloat16)


def per_device(cotangent, incident, aperture_tiles, charge, wl_index):
    rows_local = cotangent.shape[2]
    cols_local = cotangent.shape[3]
    row_first = lax.axis_index("row") * rows_local
    col_first = lax.axis_index("col") * cols_local
    extent = rows_local * lax.axis_size("row")
    size_m = M
    tile_rows = aperture_tiles.shape[0]
    tile_cols = aperture_tiles.shape[1]
    tile_size = rows_local // tile_rows
    open_tiles = (aperture_tiles == 1).astype(jnp.bfloat16)
    live_cells = jnp.broadcast_to(
        open_tiles[:, None, :, None], (tile_rows, tile_size, tile_cols, tile_size)
    ).reshape(rows_local, cols_local)
    wave_index = wl_index[0]
    norm_fwd = 1.0 / math.sqrt(extent)
    norm_back = 1.0 / math.sqrt(size_m)
    contract_first = (((0,), (0,)), ((), ()))
    col_phase = phase_grid(col_first, cols_local, extent, size_m, wave_index, False)
    fwd_cols = (
        jnp.concatenate([jnp.cos(col_phase), jnp.sin(col_phase)], axis=1) * norm_fwd
    ).astype(jnp.bfloat16)
    grad_re = cotangent[0, 0] * live_cells
    grad_im = cotangent[0, 1] * live_cells
    prod_re = jnp.dot(grad_re, fwd_cols, preferred_element_type=jnp.float32)
    prod_im = jnp.dot(grad_im, fwd_cols, preferred_element_type=jnp.float32)
    inner = jnp.concatenate(
        [prod_re[:, :size_m] - prod_im[:, size_m:], prod_re[:, size_m:] + prod_im[:, :size_m]],
        axis=1,
    ).astype(jnp.bfloat16)
    row_phase = phase_grid(row_first, rows_local, extent, size_m, wave_index, False)
    row_cos = jnp.cos(row_phase)
    row_sin = jnp.sin(row_phase)
    fwd_rcos = (row_cos * norm_fwd).astype(jnp.bfloat16)
    fwd_rsin = (row_sin * norm_fwd).astype(jnp.bfloat16)
    back_rcos = (row_cos * norm_back).astype(jnp.bfloat16)
    back_rsin = (row_sin * norm_back).astype(jnp.bfloat16)
    cos_part = fwd_rcos
    sin_part = fwd_rsin
    with_cos = lax.dot_general(cos_part, inner, contract_first, preferred_element_type=jnp.float32)
    with_sin = lax.dot_general(sin_part, inner, contract_first, preferred_element_type=jnp.float32)
    shared = lax.psum(
        jnp.concatenate(
            [
                with_cos[:, :size_m] - with_sin[:, size_m:],
                with_cos[:, size_m:] + with_sin[:, :size_m],
            ],
            axis=1,
        ),
        ("row", "col"),
    )
    turned = vortex(shared[:, :size_m], shared[:, size_m:], charge[0])
    cos_part = back_rcos
    sin_part = back_rsin
    first_part = jnp.dot(cos_part, turned, preferred_element_type=jnp.float32)
    second_part = jnp.dot(sin_part, turned, preferred_element_type=jnp.float32)
    pupil_focal = jnp.concatenate(
        [
            first_part[:, :size_m] + second_part[:, size_m:],
            first_part[:, size_m:] - second_part[:, :size_m],
        ],
        axis=1,
    )
    back_y = pupil_focal.astype(jnp.bfloat16)
    col_back = phase_grid(col_first, cols_local, extent, size_m, wave_index, True)
    back_cols = (
        jnp.concatenate([jnp.cos(col_back), jnp.sin(col_back)], axis=0) * norm_back
    ).astype(jnp.bfloat16)
    back_real = jnp.dot(back_y, back_cols, preferred_element_type=jnp.float32)
    wave_term = (
        back_real * incident[0].astype(jnp.float32) * live_cells.astype(jnp.float32)
    ).astype(jnp.bfloat16)
    summed = lax.psum(wave_term, "wl").astype(jnp.float32)
    return summed.astype(jnp.bfloat16)


def solution(mesh):
    return jax.shard_map(
        per_device,
        mesh=mesh,
        in_specs=(
            P("wl", None, "row", "col"),
            P("wl", "row", "col"),
            P("row", "col"),
            P("wl"),
            P("wl"),
        ),
        out_specs=P("row", "col"),
        check_vma=False,
    )
```

profile of v0, /device:TPU:0, one launch (start us, length us, event | category | flops | bytes accessed | tf_op | source)
XLA Modules:
  0.0 437.1 jit_solution(7436106996927162927)
XLA Ops:
  7.2 0.7 compare_convert_fusion
  8.0 64.3 %fusion.22 = (f32[2048,512]{1,0:T(8,128)S(1)}, f32[2048,512]{1,0:T(8,128)S(1)}) fusion(f32[]{:T(128)S(6)} %div.2, s32[]{:T(128)S(6)} %select_n.21, s32[512]{0:T(512)S(1)} %multiply_add_fusion.2, s32[2048]{0:T(1024)S(1)} %multiply_add_fusion, pred[]{:T(512)S(6)} %lt.21), kind=kLoop, calls=%fused_computation.30 | loop fusion | flops 11534336 | bytes 8398857 | tf_op jit(solution)/shard_map/cos | solution.py:55
  72.3 0.6 broadcast_in_dim.2
  72.9 10.3 %fusion.9 = f32[1024,1024]{0,1:T(8,128)} fusion(bf16[1,2,1024,2048]{3,2,1,0:T(8,128)(2,1)} %param.5, bf16[128,8,16,128]{3,2,1,0:T(8,128)(2,1)S(1)} %bitcast.23, f32[2048,512]{1,0:T(8,128)S(1)} %get-tuple-element.14, f32[2048,512]{1,0:T(8,128)S(1)} %get-tuple-element.13), kind=kOutput, calls=%fused_computation.15 | convolution fusion | flops 4303355904 | bytes 20971520 | tf_op jit(solution)/shard_map/dot_general | solution.py:59
  83.3 8.9 %fusion.10 = f32[1024,1024]{0,1:T(8,128)} fusion(bf16[1,2,1024,2048]{3,2,1,0:T(8,128)(2,1)} %param.5, bf16[128,8,16,128]{3,2,1,0:T(8,128)(2,1)S(1)} %bitcast.24, f32[2048,512]{1,0:T(8,128)S(1)} %get-tuple-element.14, f32[2048,512]{1,0:T(8,128)S(1)} %get-tuple-element.13), kind=kOutput, calls=%fused_computation.16 | convolution fusion | flops 4303355904 | bytes 20971520 | tf_op jit(solution)/shard_map/dot_general | solution.py:60
  92.2 4.2 fusion.35
  96.4 28.7 %fusion.46 = f32[512,1024]{1,0:T(8,128)S(1)} fusion(bf16[1024,512]{0,1:T(8,128)(2,1)S(1)} %get-tuple-element.8, bf16[1024,512]{0,1:T(8,128)(2,1)S(1)} %get-tuple-element.7, f32[]{:T(128)S(6)} %div.2, s32[]{:T(128)S(6)} %select_n.21, s32[512]{0:T(512)S(1)} %multiply_add_fusion.2, s32[1024]{0:T(1024)S(1)} %multiply_add_fusion.1, pred[]{:T(512)S(6)} %lt.21), kind=kOutput, calls=%fused_computation.66 | convolution fusion | flops 1084751872 | bytes 4200457 | tf_op jit(solution)/shard_map/dot_general | solution.py:74
  125.0 28.5 %fusion.45 = f32[512,1024]{1,0:T(8,128)S(1)} fusion(bf16[1024,512]{0,1:T(8,128)(2,1)S(1)} %get-tuple-element.8, bf16[1024,512]{0,1:T(8,128)(2,1)S(1)} %get-tuple-element.7, f32[]{:T(128)S(6)} %div.2, s32[]{:T(128)S(6)} %select_n.21, s32[512]{0:T(512)S(1)} %multiply_add_fusion.2, s32[1024]{0:T(1024)S(1)} %multiply_add_fusion.1, pred[]{:T(512)S(6)} %lt.21), kind=kOutput, calls=%fused_computation.65 | convolution fusion | flops 1084751872 | bytes 4200457 | tf_op jit(solution)/shard_map/dot_general | solution.py:75
  153.6 0.5 slice_subtract_fusion.2
  154.1 1.5 pad_maximum_fusion.1
  155.5 0.0 all-reduce.3.cloned.1.call-update
  155.6 0.0 all-reduce.5.cloned.1.call-start
  156.3 58.1 %fusion.17 = (f32[512,2048]{1,0:T(8,128)}, f32[512,2048]{1,0:T(8,128)}) fusion(f32[]{:T(128)S(6)} %div.2, s32[]{:T(128)S(6)} %select_n.21, s32[2048]{0:T(1024)S(1)} %multiply_add_fusion, s32[512]{0:T(512)S(1)} %multiply_add_fusion.2, pred[]{:T(512)S(6)} %lt.21), kind=kLoop, calls=%fused_computation.24 | loop fusion | flops 11534336 | bytes 8398857 | tf_op jit(solution)/shard_map/cos | solution.py:101
  214.3 46.3 %all-reduce.3.cloned.1.call-done = f32[512,1024]{1,0:T(8,128)} async-done(((f32[512,1024]{1,0:T(8,128)}), f32[512,1024]{1,0:T(8,128)}) %all-reduce.3.cloned.1.call-update) | async-done | bytes 2097168 | tf_op jit(solution)/shard_map/psum | solution.py:76
  260.6 8.1 %add_convert_fusion = (bf16[512,512]{1,0:T(8,128)(2,1)S(1)}, bf16[512,512]{1,0:T(8,128)(2,1)S(1)}) fusion(f32[512,1024]{1,0:T(8,128)} %all-reduce.3.cloned.1.call-done, f32[]{:T(128)} %bitcast.3, f32[512]{0:T(512)S(1)} %fusion.81), kind=kLoop, calls=%fused_computation.73 | loop fusion | flops 2359296 | bytes 3149828 | tf_op jit(solution)/shard_map/convert.3
  268.7 28.2 %fusion.47 = f32[1024,1024]{0,1:T(8,128)S(1)} fusion(f32[]{:T(128)S(6)} %div.2, s32[]{:T(128)S(6)} %select_n.21, s32[512]{0:T(512)S(1)} %multiply_add_fusion.2, s32[1024]{0:T(1024)S(1)} %multiply_add_fusion.1, pred[]{:T(512)S(6)} %lt.21, bf16[512,512]{1,0:T(8,128)(2,1)S(1)} %get-tuple-element.12, bf16[512,512]{1,0:T(8,128)(2,1)S(1)} %get-tuple-element.11), kind=kOutput, calls=%fused_computation.67 | convolution fusion | flops 1082654720 | bytes 5249033 | tf_op jit(solution)/shard_map/dot_general | solution.py:89
  297.0 28.5 %fusion.48 = f32[1024,1024]{0,1:T(8,128)S(1)} fusion(f32[]{:T(128)S(6)} %div.2, s32[]{:T(128)S(6)} %select_n.21, s32[512]{0:T(512)S(1)} %multiply_add_fusion.2, s32[1024]{0:T(1024)S(1)} %multiply_add_fusion.1, pred[]{:T(512)S(6)} %lt.21, bf16[512,512]{1,0:T(8,128)(2,1)S(1)} %get-tuple-element.12, bf16[512,512]{1,0:T(8,128)(2,1)S(1)} %get-tuple-element.11), kind=kOutput, calls=%fused_computation.68 | convolution fusion | flops 1082654720 | bytes 5249033 | tf_op jit(solution)/shard_map/dot_general | solution.py:90
  325.5 2.1 fusion.33
  327.6 0.8 copy-done.1
  328.4 1.3 copy-done.2
  329.7 10.6 %fusion.3 = bf16[1024,2048]{1,0:T(8,128)(2,1)} fusion(f32[512,2048]{1,0:T(8,128)S(1)} %copy-done.3, f32[512,2048]{1,0:T(8,128)S(1)} %copy-done.2, bf16[1,1024,2048]{2,1,0:T(8,128)(2,1)} %param.6, bf16[128,8,16,128]{3,2,1,0:T(8,128)(2,1)S(1)} %bitcast.25, bf16[1024,512]{0,1:T(8,128)(2,1)} %get-tuple-element.6, bf16[1024,512]{0,1:T(8,128)(2,1)} %get-tuple-element.5), kind=kOutput, calls=%fused_computation.6 | convolution fusion | flops 4315938816 | bytes 23068672 | tf_op jit(solution)/shard_map/dot_general | solution.py:103
  340.3 0.0 all-reduce.5.cloned.1.call-update
  340.3 84.9 %all-reduce.5.cloned.1.call-done = bf16[1024,2048]{1,0:T(8,128)(2,1)} async-done(((bf16[1024,2048]{1,0:T(8,128)(2,1)}), bf16[1024,2048]{1,0:T(8,128)(2,1)}) %all-reduce.5.cloned.1.call-update) | async-done | bytes 4194320 | tf_op jit(solution)/shard_map/psum | solution.py:107
  425.2 4.8 %copy.20 = bf16[1024,2048]{1,0:T(8,128)(2,1)} copy(bf16[1024,2048]{1,0:T(8,128)(2,1)} %all-reduce.5.cloned.1.call-done) | data formatting | bytes 8388608
  (11 shorter events, 0.0 us)
Async XLA Ops:
  6.5 254.1 %all-reduce.3.cloned.1.call-start = ((), (), s32[]{:S(2)}) async-start(), calls=%async_computation | async-start | bytes 4194304 | tf_op jit(solution)/shard_map/psum | solution.py:76
  72.9 10.4 %copy-start = (bf16[8,128,16,128]{3,2,1,0:T(8,128)(2,1)}, bf16[8,128,16,128]{3,2,1,0:T(8,128)(2,1)S(1)}, u32[]{:S(2)}) copy-start(bf16[8,128,16,128]{3,2,1,0:T(8,128)(2,1)S(1)} %broadcast_in_dim.2) | copy-start | bytes 12582916
  155.6 269.7 %all-reduce.5.cloned.1.call-start = ((), (), s32[]{:S(2)}) async-start(), calls=%async_computation.1 | async-start | bytes 8388608 | tf_op jit(solution)/shard_map/psum | solution.py:107
  297.0 30.6 %copy-start.3 = (f32[512,2048]{1,0:T(8,128)S(1)}, f32[512,2048]{1,0:T(8,128)}, u32[]{:S(2)}) copy-start(f32[512,2048]{1,0:T(8,128)} %get-tuple-element.16) | copy-start | bytes 12582916
  325.4 2.9 copy-start.1
  325.5 4.2 copy-start.2
Sparse Core Ops, SparseCore 0:
  155.7 104.9 all-reduce.2
  340.4 84.7 all-reduce.4
where the time goes:
time: 438 us; the launch traced here: 437 us
  matrix products  144 us (33%)
  other arithmetic  140 us (32%)
  waiting for transfers between devices  131 us (30%)
  between operations  15.2 us (3%)
  local copies, waits for them, and re-layouts  7.49 us (2%)
    psum x1, waiting for transfers between devices, per_device(): summed = lax.psum(wave_term, 'wl').astype(jnp.float32)  84.9 us
    cos x1, other arithmetic, per_device(): jnp.cos(col_phase)  64.3 us
    cos x1, other arithmetic, per_device(): jnp.cos(col_back)  58.1 us
    psum x1, waiting for transfers between devices, per_device(): lax.psum(jnp.concatenate([with_cos[:, :size_m] - with_sin[:, size_m:], wi...  46.3 us
    dot_general x1, matrix products, per_device(): lax.dot_general(cos_part, inner, contract_first, preferred_element_type=j...  28.7 us
    dot_general x1, matrix products, per_device(): lax.dot_general(sin_part, inner, contract_first, preferred_element_type=j...  28.5 us
    dot_general x1, matrix products, per_device(): second_part = jnp.dot(sin_part, turned, preferred_element_type=jnp.float32)  28.5 us
    dot_general x1, matrix products, per_device(): first_part = jnp.dot(cos_part, turned, preferred_element_type=jnp.float32)  28.2 us
  transfers between devices with their start and end apart: 2, of which 2 were waited for; matrix products, arithmetic and copies ran while one was open for 13% of the time, Pallas kernels for 0%

commit v1 on v0

--- a/solution.py
+++ b/solution.py
@@ -73,16 +73,12 @@
     sin_part = fwd_rsin
     with_cos = lax.dot_general(cos_part, inner, contract_first, preferred_element_type=jnp.float32)
     with_sin = lax.dot_general(sin_part, inner, contract_first, preferred_element_type=jnp.float32)
-    shared = lax.psum(
-        jnp.concatenate(
-            [
-                with_cos[:, :size_m] - with_sin[:, size_m:],
-                with_cos[:, size_m:] + with_sin[:, :size_m],
-            ],
-            axis=1,
-        ),
-        ("row", "col"),
+    shared = jnp.concatenate(
+        [with_cos[:, :size_m] - with_sin[:, size_m:], with_cos[:, size_m:] + with_sin[:, :size_m]],
+        axis=1,
     )
+    for over in ("col", "row"):
+        shared = lax.psum(shared, over)
     turned = vortex(shared[:, :size_m], shared[:, size_m:], charge[0])
     cos_part = back_rcos
     sin_part = back_rsin

time: 438 us -> 486 us (1.11)
  waiting for transfers between devices: 131 us -> 180 us
    psum x1 -> x2, waiting for transfers between devices: 46.3 us -> 95.5 us  [per_device(): shared = lax.psum(shared, over)]
  transfers between devices with their start and end apart: 2 -> 3, of which waited for: 2 -> 3; matrix products, arithmetic and copies ran while one was open for 13% -> 12% of each run, Pallas kernels for 0% -> 0%
where the time goes in v1:
time: 486 us
  waiting for transfers between devices  180 us (37%)
  matrix products  144 us (30%)
  other arithmetic  139 us (29%)
  between operations  14.9 us (3%)
  local copies, waits for them, and re-layouts  7.49 us (2%)
    psum x2, waiting for transfers between devices, per_device(): shared = lax.psum(shared, over)  95.5 us
    psum x1, waiting for transfers between devices, per_device(): summed = lax.psum(wave_term, 'wl').astype(jnp.float32)  84.7 us
    cos x1, other arithmetic, per_device(): jnp.cos(col_phase)  64.3 us
    cos x1, other arithmetic, per_device(): jnp.cos(col_back)  58.1 us
    dot_general x1, matrix products, per_device(): lax.dot_general(cos_part, inner, contract_first, preferred_element_type=j...  28.7 us
    dot_general x1, matrix products, per_device(): lax.dot_general(sin_part, inner, contract_first, preferred_element_type=j...  28.5 us
    dot_general x1, matrix products, per_device(): second_part = jnp.dot(sin_part, turned, preferred_element_type=jnp.float32)  28.5 us
    dot_general x1, matrix products, per_device(): first_part = jnp.dot(cos_part, turned, preferred_element_type=jnp.float32)  28.2 us
  transfers between devices with their start and end apart: 3, of which 3 were waited for; matrix products, arithmetic and copies ran while one was open for 12% of the time, Pallas kernels for 0%

profile of v1, /device:TPU:0, one launch (start us, length us, event | category | flops | bytes accessed | tf_op | source)
XLA Modules:
  0.0 485.9 jit_solution(1383664181652944255)
XLA Ops:
  7.2 0.7 compare_convert_fusion
  8.0 64.3 %fusion.22 = (f32[2048,512]{1,0:T(8,128)S(1)}, f32[2048,512]{1,0:T(8,128)S(1)}) fusion(f32[]{:T(128)S(6)} %div.2, s32[]{:T(128)S(6)} %select_n.21, s32[512]{0:T(512)S(1)} %multiply_add_fusion.2, s32[2048]{0:T(1024)S(1)} %multiply_add_fusion, pred[]{:T(512)S(6)} %lt.21), kind=kLoop, calls=%fused_computation.30 | loop fusion | flops 11534336 | bytes 8398857 | tf_op jit(solution)/shard_map/cos | solution.py:55
  72.3 0.6 broadcast_in_dim.2
  72.9 10.3 %fusion.9 = f32[1024,1024]{0,1:T(8,128)} fusion(bf16[1,2,1024,2048]{3,2,1,0:T(8,128)(2,1)} %param.5, bf16[128,8,16,128]{3,2,1,0:T(8,128)(2,1)S(1)} %bitcast.23, f32[2048,512]{1,0:T(8,128)S(1)} %get-tuple-element.14, f32[2048,512]{1,0:T(8,128)S(1)} %get-tuple-element.13), kind=kOutput, calls=%fused_computation.15 | convolution fusion | flops 4303355904 | bytes 20971520 | tf_op jit(solution)/shard_map/dot_general | solution.py:59
  83.3 8.9 %fusion.10 = f32[1024,1024]{0,1:T(8,128)} fusion(bf16[1,2,1024,2048]{3,2,1,0:T(8,128)(2,1)} %param.5, bf16[128,8,16,128]{3,2,1,0:T(8,128)(2,1)S(1)} %bitcast.24, f32[2048,512]{1,0:T(8,128)S(1)} %get-tuple-element.14, f32[2048,512]{1,0:T(8,128)S(1)} %get-tuple-element.13), kind=kOutput, calls=%fused_computation.16 | convolution fusion | flops 4303355904 | bytes 20971520 | tf_op jit(solution)/shard_map/dot_general | solution.py:60
  92.2 4.2 fusion.35
  96.4 28.7 %fusion.46 = f32[512,1024]{1,0:T(8,128)S(1)} fusion(bf16[1024,512]{0,1:T(8,128)(2,1)S(1)} %get-tuple-element.8, bf16[1024,512]{0,1:T(8,128)(2,1)S(1)} %get-tuple-element.7, f32[]{:T(128)S(6)} %div.2, s32[]{:T(128)S(6)} %select_n.21, s32[512]{0:T(512)S(1)} %multiply_add_fusion.2, s32[1024]{0:T(1024)S(1)} %multiply_add_fusion.1, pred[]{:T(512)S(6)} %lt.21), kind=kOutput, calls=%fused_computation.66 | convolution fusion | flops 1084751872 | bytes 4200457 | tf_op jit(solution)/shard_map/dot_general | solution.py:74
  125.0 28.5 %fusion.45 = f32[512,1024]{1,0:T(8,128)S(1)} fusion(bf16[1024,512]{0,1:T(8,128)(2,1)S(1)} %get-tuple-element.8, bf16[1024,512]{0,1:T(8,128)(2,1)S(1)} %get-tuple-element.7, f32[]{:T(128)S(6)} %div.2, s32[]{:T(128)S(6)} %select_n.21, s32[512]{0:T(512)S(1)} %multiply_add_fusion.2, s32[1024]{0:T(1024)S(1)} %multiply_add_fusion.1, pred[]{:T(512)S(6)} %lt.21), kind=kOutput, calls=%fused_computation.65 | convolution fusion | flops 1084751872 | bytes 4200457 | tf_op jit(solution)/shard_map/dot_general | solution.py:75
  153.6 0.5 slice_subtract_fusion.2
  154.1 1.5 pad_maximum_fusion.1
  155.5 0.0 all-reduce.6.cloned.1.call-start
  155.6 65.8 %all-reduce.4.cloned.1.call-done = f32[512,1024]{1,0:T(8,128)} async-done(((f32[512,1024]{1,0:T(8,128)}), f32[512,1024]{1,0:T(8,128)}) %all-reduce.4.cloned.1.call-update) | async-done | bytes 2097168 | tf_op jit(solution)/shard_map/psum | solution.py:81
  221.4 0.0 all-reduce.8.cloned.1.call-start
  222.1 58.1 %fusion.17 = (f32[512,2048]{1,0:T(8,128)}, f32[512,2048]{1,0:T(8,128)}) fusion(f32[]{:T(128)S(6)} %div.2, s32[]{:T(128)S(6)} %select_n.21, s32[2048]{0:T(1024)S(1)} %multiply_add_fusion, s32[512]{0:T(512)S(1)} %multiply_add_fusion.2, pred[]{:T(512)S(6)} %lt.21), kind=kLoop, calls=%fused_computation.24 | loop fusion | flops 11534336 | bytes 8398857 | tf_op jit(solution)/shard_map/cos | solution.py:97
  280.2 29.7 %all-reduce.6.cloned.1.call-done = f32[512,1024]{1,0:T(8,128)} async-done(((f32[512,1024]{1,0:T(8,128)}), f32[512,1024]{1,0:T(8,128)}) %all-reduce.6.cloned.1.call-update) | async-done | bytes 2097168 | tf_op jit(solution)/shard_map/psum | solution.py:81
  309.9 8.1 %add_convert_fusion = (bf16[512,512]{1,0:T(8,128)(2,1)S(1)}, bf16[512,512]{1,0:T(8,128)(2,1)S(1)}) fusion(f32[512,1024]{1,0:T(8,128)} %all-reduce.6.cloned.1.call-done, f32[]{:T(128)} %bitcast.3, f32[512]{0:T(512)S(1)} %fusion.81), kind=kLoop, calls=%fused_computation.73 | loop fusion | flops 2359296 | bytes 3149828 | tf_op jit(solution)/shard_map/convert.3
  318.1 28.2 %fusion.47 = f32[1024,1024]{0,1:T(8,128)S(1)} fusion(f32[]{:T(128)S(6)} %div.2, s32[]{:T(128)S(6)} %select_n.21, s32[512]{0:T(512)S(1)} %multiply_add_fusion.2, s32[1024]{0:T(1024)S(1)} %multiply_add_fusion.1, pred[]{:T(512)S(6)} %lt.21, bf16[512,512]{1,0:T(8,128)(2,1)S(1)} %get-tuple-element.12, bf16[512,512]{1,0:T(8,128)(2,1)S(1)} %get-tuple-element.11), kind=kOutput, calls=%fused_computation.67 | convolution fusion | flops 1082654720 | bytes 5249033 | tf_op jit(solution)/shard_map/dot_general | solution.py:85
  346.3 28.5 %fusion.48 = f32[1024,1024]{0,1:T(8,128)S(1)} fusion(f32[]{:T(128)S(6)} %div.2, s32[]{:T(128)S(6)} %select_n.21, s32[512]{0:T(512)S(1)} %multiply_add_fusion.2, s32[1024]{0:T(1024)S(1)} %multiply_add_fusion.1, pred[]{:T(512)S(6)} %lt.21, bf16[512,512]{1,0:T(8,128)(2,1)S(1)} %get-tuple-element.12, bf16[512,512]{1,0:T(8,128)(2,1)S(1)} %get-tuple-element.11), kind=kOutput, calls=%fused_computation.68 | convolution fusion | flops 1082654720 | bytes 5249033 | tf_op jit(solution)/shard_map/dot_general | solution.py:86
  374.8 2.1 fusion.33
  376.9 0.8 copy-done.1
  377.7 1.3 copy-done.2
  379.0 10.6 %fusion.3 = bf16[1024,2048]{1,0:T(8,128)(2,1)} fusion(f32[512,2048]{1,0:T(8,128)S(1)} %copy-done.3, f32[512,2048]{1,0:T(8,128)S(1)} %copy-done.2, bf16[1,1024,2048]{2,1,0:T(8,128)(2,1)} %param.6, bf16[128,8,16,128]{3,2,1,0:T(8,128)(2,1)S(1)} %bitcast.25, bf16[1024,512]{0,1:T(8,128)(2,1)} %get-tuple-element.6, bf16[1024,512]{0,1:T(8,128)(2,1)} %get-tuple-element.5), kind=kOutput, calls=%fused_computation.6 | convolution fusion | flops 4315938816 | bytes 23068672 | tf_op jit(solution)/shard_map/dot_general | solution.py:99
  389.6 84.7 %all-reduce.8.cloned.1.call-done = bf16[1024,2048]{1,0:T(8,128)(2,1)} async-done(((bf16[1024,2048]{1,0:T(8,128)(2,1)}), bf16[1024,2048]{1,0:T(8,128)(2,1)}) %all-reduce.8.cloned.1.call-update) | async-done | bytes 4194320 | tf_op jit(solution)/shard_map/psum | solution.py:103
  474.3 4.8 copy.21
  (14 shorter events, 0.1 us)
Async XLA Ops:
  6.5 214.9 %all-reduce.4.cloned.1.call-start = ((), (), s32[]{:S(2)}) async-start(), calls=%async_computation | async-start | bytes 4194304 | tf_op jit(solution)/shard_map/psum | solution.py:81
  72.9 10.4 %copy-start = (bf16[8,128,16,128]{3,2,1,0:T(8,128)(2,1)}, bf16[8,128,16,128]{3,2,1,0:T(8,128)(2,1)S(1)}, u32[]{:S(2)}) copy-start(bf16[8,128,16,128]{3,2,1,0:T(8,128)(2,1)S(1)} %broadcast_in_dim.2) | copy-start | bytes 12582916
  155.5 154.4 %all-reduce.6.cloned.1.call-start = ((), (), s32[]{:S(2)}) async-start(), calls=%async_computation.1 | async-start | bytes 4194304 | tf_op jit(solution)/shard_map/psum | solution.py:81
  221.4 252.9 %all-reduce.8.cloned.1.call-start = ((), (), s32[]{:S(2)}) async-start(), calls=%async_computation.2 | async-start | bytes 8388608 | tf_op jit(solution)/shard_map/psum | solution.py:103
  346.3 30.6 %copy-start.3 = (f32[512,2048]{1,0:T(8,128)S(1)}, f32[512,2048]{1,0:T(8,128)}, u32[]{:S(2)}) copy-start(f32[512,2048]{1,0:T(8,128)} %get-tuple-element.16) | copy-start | bytes 12582916
  374.8 2.9 copy-start.1
  374.8 4.2 copy-start.2
Sparse Core Ops, SparseCore 0:
  155.7 65.6 all-reduce.3
  223.7 86.1 all-reduce.5
  389.7 84.5 all-reduce.7
